TPU v7x, 32 devices: a whole 2x2x4 slice. The times are simulated.
32 devices in a mesh: dp: 16 (over z, y, core), tensor: 2 (over x).
Axes of the slice: x: 2, y: 2, z: 4, core: 2. Of those that a mesh axis runs over, the one named last changes fastest.
Arguments:
- tokens: bfloat16 [32768, 768], P('dp'), may hold values from -6 to 6
- qkv_weight: bfloat16 [768, 3, 768], P(None, None, 'tensor'), may hold values from -0.21875 to 0.21875
- qv_bias: float32 [2, 768], P(None, 'tensor'), may hold values from -1.5 to 1.5
- proj_weight: bfloat16 [768, 768], P('tensor'), may hold values from -1.75 to 1.75
- proj_bias: float32 [768], replicated, may hold values from -1.5 to 1.5
- first_gain: float32 [768], replicated, may hold values from 0.5 to 1.5
- first_shift: float32 [768], replicated, may hold values from -1.5 to 1.5
- up_weight: bfloat16 [768, 3072], P(None, 'tensor'), may hold values from -0.21875 to 0.21875
- up_bias: float32 [3072], P('tensor'), may hold values from -1.5 to 1.5
- down_weight: bfloat16 [3072, 768], P('tensor'), may hold values from -0.109375 to 0.109375
- down_bias: float32 [768], replicated, may hold values from -1.5 to 1.5
- second_gain: float32 [768], replicated, may hold values from 0.5 to 1.5
- second_shift: float32 [768], replicated, may hold values from -1.5 to 1.5
- cotangent: bfloat16 [32768, 768], P('dp'), may hold values from -6 to 6
- bucket: int32 [16], P('dp'), may hold values from 0 to 1, as said below
- lengths: int32 [256], P('dp'), may hold values from 0 to 512, as said below
- dropped: int32 [256], P('dp'), may hold values 0 or 1
Outputs:
- result: bfloat16 [32768, 768], P('dp')
- tokens_grad: float32 [32768, 768], P('dp')
- qkv_weight_grad: float32 [768, 3, 768], P(None, None, 'tensor')
- qv_bias_grad: float32 [2, 768], P(None, 'tensor')
- proj_weight_grad: float32 [768, 768], P('tensor')
- proj_bias_grad: float32 [768], replicated
- first_gain_grad: float32 [768], replicated
- first_shift_grad: float32 [768], replicated
- up_weight_grad: float32 [768, 3072], P(None, 'tensor')
- up_bias_grad: float32 [3072], P('tensor')
- down_weight_grad: float32 [3072, 768], P('tensor')
- down_bias_grad: float32 [768], replicated
- second_gain_grad: float32 [768], replicated
- second_shift_grad: float32 [768], replicated
Inputs may be any that keep to these rules, and one draw needn't show every extreme that they name: Exactly a third of the token blocks, rounded down, have bucket 1. Slot k of block r (lengths[r * 16 + k]): in a block of bucket 1 every slot holds 32 to 128; in a block of bucket 0 slots k < 4 hold 128 to 512 and the other slots 0; in every block one used slot holds its whole span.
All inputs are finite; a program needn't handle non-finite values. No bound on the sum of `dropped` on one device may be relied on, other than what follows from the above.
Results may differ from a plain program's by a relative error of at most 0.015.
The roundings to bfloat16 on the way count: a program that leaves them out, or rounds other values in their place, can miss the bound.
Values may be sent and summed in bfloat16 or wider, within the bound.
No kernel may reach another device: no remote copies, remote signals or barrier semaphores. Data moves between devices by JAX's collectives and lax.ppermute only.
A program may use at most 192 MiB of HBM per device.

v0:
```python
import math
import jax
import jax.numpy as jnp
from jax import lax
from jax.sharding import PartitionSpec as P

HEAD = 64
LONG = 512
SHORT = 128


def dot_last(left, right):
    return lax.dot_general(
        left, right, (((1,), (1,)), ((), ())), preferred_element_type=jnp.float32
    )


def dot_first(left, right):
    return lax.dot_general(
        left, right, (((0,), (0,)), ((), ())), preferred_element_type=jnp.float32
    )


def layout(bucket, lengths, dropped, token_count):
    position = jnp.arange(token_count, dtype=jnp.int32)
    seq_span = jnp.where(bucket[0] == 1, SHORT, LONG).astype(jnp.int32)
    slot_index = position // seq_span
    offset = position % seq_span
    picker = slot_index[:, None] == jnp.arange(lengths.shape[0], dtype=jnp.int32)[None, :]
    token_length = jnp.sum(jnp.where(picker, lengths[None, :], 0), axis=1)
    token_drop = jnp.sum(jnp.where(picker, dropped[None, :], 0), axis=1)
    is_valid = offset < token_length
    keep_rows = is_valid & (token_drop == 0)
    block_count = token_count // LONG
    block_slot = slot_index.reshape(block_count, LONG)
    block_valid = is_valid.reshape(block_count, LONG)
    allowed = (block_slot[:, :, None] == block_slot[:, None, :]) & block_valid[:, None, :]
    return (keep_rows, allowed)


def norm_forward(values, gain_vec, shift_vec):
    centered = values - jnp.mean(values, axis=-1, keepdims=True)
    variance = jnp.mean(centered * centered, axis=-1, keepdims=True)
    inverse = lax.rsqrt(variance + 1e-05)
    scaled = centered * inverse
    return (scaled * gain_vec + shift_vec, scaled, inverse)


def norm_backward(upstream, scaled, inverse, gain_vec):
    gain_grad = jnp.sum(upstream * scaled, axis=0)
    shift_grad = jnp.sum(upstream, axis=0)
    through = upstream * gain_vec
    inner_part = (
        through
        - jnp.mean(through, axis=-1, keepdims=True)
        - scaled * jnp.mean(through * scaled, axis=-1, keepdims=True)
    )
    return (inner_part * inverse, gain_grad, shift_grad)


def gelu_slope(values):
    cumulative = 0.5 * (1.0 + lax.erf(values * (1.0 / math.sqrt(2.0))))
    density = jnp.exp(-0.5 * values * values) * (1.0 / math.sqrt(2.0 * math.pi))
    return cumulative + values * density


def block_scores(query_blk, key_blk, allowed_blk):
    row_count = query_blk.shape[0]
    head_split = (row_count, query_blk.shape[1] // HEAD, HEAD)
    scores = jnp.einsum(
        "qhd,khd->hqk",
        query_blk.reshape(head_split),
        key_blk.reshape(head_split),
        preferred_element_type=jnp.float32,
    ) * (1.0 / math.sqrt(HEAD))
    return (jnp.where(allowed_blk[None], scores, -1e30), head_split)


def attend_block(operands):
    query_blk, key_blk, value_blk, allowed_blk = operands
    scores, head_split = block_scores(query_blk, key_blk, allowed_blk)
    row_max = jnp.max(scores, axis=-1, keepdims=True)
    exp_scores = jnp.exp(scores - row_max)
    row_sum = jnp.sum(exp_scores, axis=-1, keepdims=True)
    prob_rows = exp_scores / row_sum
    context = jnp.einsum(
        "hqk,khd->qhd",
        prob_rows.astype(jnp.bfloat16),
        value_blk.reshape(head_split),
        preferred_element_type=jnp.float32,
    )
    context = context.reshape(query_blk.shape[0], -1).astype(jnp.bfloat16)
    log_total = row_max[..., 0] + jnp.log(row_sum[..., 0])
    return (context, log_total)


def attend_back(operands):
    query_blk, key_blk, value_blk, allowed_blk, log_total, grad_ctx = operands
    scores, head_split = block_scores(query_blk, key_blk, allowed_blk)
    prob_rows = jnp.exp(scores - log_total[..., None])
    prob_low = prob_rows.astype(jnp.bfloat16)
    grad_ctx_heads = grad_ctx.reshape(head_split)
    grad_prob = jnp.einsum(
        "qhd,khd->hqk",
        grad_ctx_heads,
        value_blk.reshape(head_split),
        preferred_element_type=jnp.float32,
    )
    row_dot = jnp.sum(prob_rows * grad_prob, axis=-1, keepdims=True)
    grad_score = (prob_rows * (grad_prob - row_dot)).astype(jnp.bfloat16)
    scale_factor = 1.0 / math.sqrt(HEAD)
    row_count = query_blk.shape[0]
    grad_query = (
        jnp.einsum(
            "hqk,khd->qhd",
            grad_score,
            key_blk.reshape(head_split),
            preferred_element_type=jnp.float32,
        )
        * scale_factor
    )
    grad_key = (
        jnp.einsum(
            "hqk,qhd->khd",
            grad_score,
            query_blk.reshape(head_split),
            preferred_element_type=jnp.float32,
        )
        * scale_factor
    )
    grad_value = jnp.einsum(
        "hqk,qhd->khd", prob_low, grad_ctx_heads, preferred_element_type=jnp.float32
    )
    return jnp.concatenate(
        [
            grad_query.reshape(row_count, -1).astype(jnp.bfloat16),
            grad_key.reshape(row_count, -1).astype(jnp.bfloat16),
            grad_value.reshape(row_count, -1).astype(jnp.bfloat16),
        ],
        axis=-1,
    )


def body(
    tokens,
    qkv_weight,
    qv_bias,
    proj_weight,
    proj_bias,
    first_gain,
    first_shift,
    up_weight,
    up_bias,
    down_weight,
    down_bias,
    second_gain,
    second_shift,
    cotangent,
    bucket,
    lengths,
    dropped,
):
    token_count, model_width = tokens.shape
    split_count = lax.axis_size("tensor")
    half_rows = token_count // split_count
    row_start = lax.axis_index("tensor") * half_rows
    block_count = token_count // LONG
    keep_rows, allowed = layout(bucket, lengths, dropped, token_count)
    local_width = qkv_weight.shape[2]
    qkv_flat = qkv_weight.reshape(model_width, 3 * local_width)
    projected = jnp.dot(tokens, qkv_flat, preferred_element_type=jnp.float32)
    bias_row = jnp.concatenate([qv_bias[0], jnp.zeros_like(qv_bias[0]), qv_bias[1]])
    qkv_low = (projected + bias_row).astype(jnp.bfloat16)
    block_view = (block_count, LONG, local_width)
    query_blocks = qkv_low[:, :local_width].reshape(block_view)
    key_blocks = qkv_low[:, local_width : 2 * local_width].reshape(block_view)
    value_blocks = qkv_low[:, 2 * local_width :].reshape(block_view)
    context, log_totals = lax.map(attend_block, (query_blocks, key_blocks, value_blocks, allowed))
    context = context.reshape(token_count, local_width)
    attn_share = lax.psum_scatter(
        jnp.dot(context, proj_weight, preferred_element_type=jnp.float32),
        "tensor",
        scatter_dimension=0,
        tiled=True,
    )
    own_tokens = lax.dynamic_slice_in_dim(tokens, row_start, half_rows, 0).astype(jnp.float32)
    first_sum = own_tokens + attn_share + proj_bias
    hidden, scaled_one, inverse_one = norm_forward(first_sum, first_gain, first_shift)
    hidden_all = lax.all_gather(hidden.astype(jnp.bfloat16), "tensor", axis=0, tiled=True)
    pre_act = jnp.dot(hidden_all, up_weight, preferred_element_type=jnp.float32) + up_bias
    activated = jax.nn.gelu(pre_act, approximate=False).astype(jnp.bfloat16)
    ffn_share = lax.psum_scatter(
        jnp.dot(activated, down_weight, preferred_element_type=jnp.float32).astype(jnp.bfloat16),
        "tensor",
        scatter_dimension=0,
        tiled=True,
    ).astype(jnp.float32)
    second_sum = hidden + ffn_share + down_bias
    normed, scaled_two, inverse_two = norm_forward(second_sum, second_gain, second_shift)
    keep_own = lax.dynamic_slice_in_dim(keep_rows, row_start, half_rows, 0)
    result_own = jnp.where(keep_own[:, None], normed, own_tokens).astype(jnp.bfloat16)
    result = lax.all_gather(result_own, "tensor", axis=0, tiled=True)
    upstream = lax.dynamic_slice_in_dim(cotangent, row_start, half_rows, 0).astype(jnp.float32)
    grad_normed = jnp.where(keep_own[:, None], upstream, 0.0)
    grad_skip = jnp.where(keep_own[:, None], 0.0, upstream)
    grad_second, gain_two_grad, shift_two_grad = norm_backward(
        grad_normed, scaled_two, inverse_two, second_gain
    )
    down_bias_grad = jnp.sum(grad_second, axis=0)
    branch_grad = lax.all_gather(grad_second.astype(jnp.bfloat16), "tensor", axis=0, tiled=True)
    down_grad = dot_first(activated, branch_grad)
    grad_act = dot_last(branch_grad, down_weight)
    grad_pre = (grad_act * gelu_slope(pre_act)).astype(jnp.bfloat16)
    up_bias_grad = jnp.sum(grad_pre, axis=0, dtype=jnp.float32)
    up_grad = dot_first(hidden_all, grad_pre)
    grad_hidden = grad_second + lax.psum_scatter(
        dot_last(grad_pre, up_weight).astype(jnp.bfloat16),
        "tensor",
        scatter_dimension=0,
        tiled=True,
    ).astype(jnp.float32)
    grad_first, gain_one_grad, shift_one_grad = norm_backward(
        grad_hidden, scaled_one, inverse_one, first_gain
    )
    proj_bias_grad = jnp.sum(grad_first, axis=0)
    attn_grad = lax.all_gather(grad_first.astype(jnp.bfloat16), "tensor", axis=0, tiled=True)
    proj_grad = dot_first(context, attn_grad)
    grad_ctx = dot_last(attn_grad, proj_weight).astype(jnp.bfloat16)
    grad_qkv = lax.map(
        attend_back,
        (query_blocks, key_blocks, value_blocks, allowed, log_totals, grad_ctx.reshape(block_view)),
    )
    grad_qkv = grad_qkv.reshape(token_count, 3 * local_width)
    qkv_grad = dot_first(tokens, grad_qkv).reshape(model_width, 3, local_width)
    qkv_sums = jnp.sum(grad_qkv, axis=0, dtype=jnp.float32).reshape(3, local_width)
    qv_bias_grad = jnp.stack([qkv_sums[0], qkv_sums[2]])
    grad_input_own = (
        grad_skip
        + grad_first
        + lax.psum_scatter(
            dot_last(grad_qkv, qkv_flat).astype(jnp.bfloat16),
            "tensor",
            scatter_dimension=0,
            tiled=True,
        ).astype(jnp.float32)
    )
    tokens_grad = lax.all_gather(
        grad_input_own.astype(jnp.bfloat16), "tensor", axis=0, tiled=True
    ).astype(grad_input_own.dtype)
    norm_sums = lax.psum(
        (
            proj_bias_grad,
            gain_one_grad,
            shift_one_grad,
            down_bias_grad,
            gain_two_grad,
            shift_two_grad,
        ),
        ("dp", "tensor"),
    )
    qkv_grad, qv_bias_grad, proj_grad, up_grad, up_bias_grad, down_grad = lax.psum(
        (qkv_grad, qv_bias_grad, proj_grad, up_grad, up_bias_grad, down_grad), "dp"
    )
    return (
        result,
        tokens_grad,
        qkv_grad,
        qv_bias_grad,
        proj_grad,
        norm_sums[0],
        norm_sums[1],
        norm_sums[2],
        up_grad,
        up_bias_grad,
        down_grad,
        norm_sums[3],
        norm_sums[4],
        norm_sums[5],
    )


def solution(mesh):
    placed = (
        P("dp", None),
        P(None, None, "tensor"),
        P(None, "tensor"),
        P("tensor", None),
        P(),
        P(),
        P(),
        P(None, "tensor"),
        P("tensor"),
        P("tensor", None),
        P(),
        P(),
        P(),
        P("dp", None),
        P("dp"),
        P("dp"),
        P("dp"),
    )
    return jax.shard_map(
        body,
        mesh=mesh,
        in_specs=placed,
        out_specs=(
            P("dp", None),
            P("dp", None),
            P(None, None, "tensor"),
            P(None, "tensor"),
            P("tensor", None),
            P(),
            P(),
            P(),
            P(None, "tensor"),
            P("tensor"),
            P("tensor", None),
            P(),
            P(),
            P(),
        ),
        check_vma=False,
    )
```

profile of v0, /device:TPU:0, one launch (start us, length us, event | category | flops | bytes accessed | tf_op | source)
XLA Modules:
  0.0 972.1 jit_solution(16050319743012541369)
XLA Ops:
  10.6 3.8 copy.62
  14.4 6.7 add_convert_fusion
  21.2 2.3 fusion.69
  23.5 2.7 copy.65
  26.2 2.7 copy.64
  28.8 2.6 copy.63
  33.7 37.3 %while.22 = (s32[]{:T(128)}, bf16[4,512,384]{2,1,0:T(8,128)(2,1)}, f32[4,6,512]{2,1,0:T(8,128)}, bf16[4,512,384]{1,2,0:T(8,128)(2,1)}, pred[4,512,512]{1,2,0:T(8...) while((s32[]{:T(128)}, bf16[4,512,384]{2,1,0:T(8,128)(2,1)}, ...), condition=%wide.region_5.6_spmd, body=%wide.region_2.5_spmd.sunk | while | flops 421721088 | bytes 25792624 | solution.py:178
  71.0 6.0 fusion.72
  77.2 79.8 %reduce-scatter.5.cloned.1.call-done = f32[1024,768]{1,0:T(8,128)} async-done(((f32[2048,768]{1,0:T(8,128)}), f32[1024,768]{1,0:T(8,128)}) %reduce-scatter.5.cloned.1.call-update) | async-done | bytes 3145744 | tf_op jit(solution)/shard_map/reduce_scatter | solution.py:180
  157.0 2.8 fusion.67
  163.3 45.1 %all-gather.6.cloned.1.call-done = bf16[2048,768]{1,0:T(8,128)(2,1)} async-done(((bf16[1024,768]{1,0:T(8,128)(2,1)}), bf16[2048,768]{1,0:T(8,128)(2,1)}) %all-gather.6.cloned.1.call-update) | async-done | bytes 3145744 | tf_op jit(solution)/shard_map/all_gather | solution.py:189
  208.3 33.2 %fusion.20 = (bf16[2048,1536]{1,0:T(8,128)(2,1)S(1)}, f32[2048,1536]{1,0:T(8,128)}) fusion(f32[1536]{0:T(1024)S(1)} %copy-done.29, bf16[2048,768]{1,0:T(8,128)(2,1)} %all-gather.6.cloned.1.call-done, bf16[768,1536]{1,0:T(8,128)(2,1)S(1)} %copy-done), kind=kOutput, calls=%fused_computation.40 | convolution fusion | flops 5039456256 | bytes 24385536 | tf_op jit(solution)/shard_map/dot_general | solution.py:190
  241.5 2.6 copy-done.30
  244.1 6.3 convolution_convert_fusion.2
  251.3 42.7 %reduce-scatter.7.cloned.1.call-done = bf16[1024,768]{1,0:T(8,128)(2,1)} async-done(((bf16[2048,768]{1,0:T(8,128)(2,1)}), bf16[1024,768]{1,0:T(8,128)(2,1)}) %reduce-scatter.7.cloned.1.call-update) | async-done | bytes 1572880 | tf_op jit(solution)/shard_map/reduce_scatter | solution.py:192
  294.0 3.5 fusion.66
  299.4 2.6 fusion.45
  302.0 3.9 fusion.64
  306.0 45.0 %all-gather.10.cloned.1.call-done = bf16[2048,768]{1,0:T(8,128)(2,1)} async-done(((bf16[1024,768]{1,0:T(8,128)(2,1)}), bf16[2048,768]{1,0:T(8,128)(2,1)}) %all-gather.10.cloned.1.call-update) | async-done | bytes 3145744 | tf_op jit(solution)/shard_map/all_gather | solution.py:210
  351.0 12.6 %convert_reduce_fusion = (f32[1536]{0:T(1024)}, bf16[2048,1536]{1,0:T(8,128)(2,1)S(1)}) fusion(f32[2048,1536]{1,0:T(8,128)} %get-tuple-element.220, f32[1536]{0:T(1024)S(1)} %copy-done.29, bf16[2048,768]{1,0:T(8,128)(2,1)} %all-gather.10.cloned.1.call-done, bf16[1536,768]{1,0:T(8,128)(2,1)} %param.30), kind=kOutput, calls=%fused_computation.47 | convolution fusion | flops 4872731136 | bytes 24391680 | tf_op jit(solution)/shard_map/dot_general | solution.py:13
  363.7 2.7 copy-done.31
  366.4 6.4 convolution_convert_fusion.1
  372.9 43.5 %reduce-scatter.9.cloned.1.call-done = bf16[1024,768]{1,0:T(8,128)(2,1)} async-done(((bf16[2048,768]{1,0:T(8,128)(2,1)}), bf16[1024,768]{1,0:T(8,128)(2,1)}) %reduce-scatter.9.cloned.1.call-update) | async-done | bytes 1572880 | tf_op jit(solution)/shard_map/reduce_scatter | solution.py:216
  416.3 3.6 multiply_reduce_fusion.1
  424.5 45.0 %all-gather.12.cloned.1.call-done = bf16[2048,768]{1,0:T(8,128)(2,1)} async-done(((bf16[1024,768]{1,0:T(8,128)(2,1)}), bf16[2048,768]{1,0:T(8,128)(2,1)}) %all-gather.12.cloned.1.call-update) | async-done | bytes 3145744 | tf_op jit(solution)/shard_map/all_gather | solution.py:226
  469.5 4.9 convolution_convert_fusion.3
  474.4 60.4 %while.23 = (s32[]{:T(128)}, bf16[4,512,1152]{1,2,0:T(8,128)(2,1)}, bf16[4,512,384]{1,2,0:T(8,128)(2,1)}, pred[4,512,512]{1,2,0:T(8,128)(4,1)}, bf16[4,512,384]{...) while((s32[]{:T(128)}, bf16[4,512,1152]{1,2,0:T(8,128)(2,1)}, ...), condition=%wide.region_19.20_spmd, body=%wide.region_17.19_spmd.sunk | while | flops 1034744832 | bytes 58806396 | solution.py:229
  482.7 2.3 multiply_reduce_fusion.7
  497.7 2.3 multiply_reduce_fusion.7
  512.7 2.3 multiply_reduce_fusion.7
  527.7 2.3 multiply_reduce_fusion.7
  534.8 6.7 copy.71
  541.5 7.9 convolution_convert_fusion
  550.3 42.7 %reduce-scatter.11.cloned.1.call-done = bf16[1024,768]{1,0:T(8,128)(2,1)} async-done(((bf16[2048,768]{1,0:T(8,128)(2,1)}), bf16[1024,768]{1,0:T(8,128)(2,1)}) %reduce-scatter.11.cloned.1.call-update) | async-done | bytes 1572880 | tf_op jit(solution)/shard_map/reduce_scatter | solution.py:240
  593.0 3.7 fusion.48
  596.8 9.9 %fusion.76 = f32[1536,768]{1,0:T(8,128)} fusion(bf16[2048,1536]{1,0:T(8,128)(2,1)} %copy-done.30, bf16[2048,768]{1,0:T(8,128)(2,1)} %all-gather.10.cloned.1.call-done), kind=kOutput, calls=%fused_computation.151 | convolution fusion | flops 4831838208 | bytes 14155776 | tf_op jit(solution)/shard_map/dot_general | solution.py:19
  606.7 9.7 %fusion.75 = f32[768,1536]{1,0:T(8,128)} fusion(bf16[2048,768]{1,0:T(8,128)(2,1)S(1)} %copy-done.27, bf16[2048,1536]{1,0:T(8,128)(2,1)} %copy-done.31), kind=kOutput, calls=%fused_computation.150 | convolution fusion | flops 4831838208 | bytes 14155776 | tf_op jit(solution)/shard_map/dot_general | solution.py:19
  616.4 4.0 fusion.73
  620.4 2.9 copy.72
  623.4 4.8 fusion.74
  628.2 11.3 %all-gather.8.cloned.1.call-done = bf16[2048,768]{1,0:T(8,128)(2,1)} async-done(((bf16[1024,768]{1,0:T(8,128)(2,1)}), bf16[2048,768]{1,0:T(8,128)(2,1)}) %all-gather.8.cloned.1.call-update) | async-done | bytes 3145744 | tf_op jit(solution)/shard_map/all_gather | solution.py:202
  639.5 40.4 %all-reduce = (f32[768]{0:T(1024)}, f32[768]{0:T(1024)}, f32[768]{0:T(1024)}, f32[768]{0:T(1024)}, f32[768]{0:T(1024)}, /*index=5*/f32[768]{0:T(1024)}) all-reduce(f32[768]{0:T(1024)S(1)} %get-tuple-element.197, f32[768]{0:T(1024)S(1)} %get-tuple-element.142, ...), channel_id=1, replica_groups=mesh['dp'=16,'tensor'=2] {'dp','tensor'}, use_global_device_ids=true, to_apply=%region_26.27 | all-reduce | flops 4608 | bytes 36864 | tf_op jit(solution)/shard_map/psum | solution.py:250
  679.9 3.0 convert_reduce_fusion.1
  683.0 63.2 %all-reduce.1 = (f32[2,384]{1,0:T(2,128)}, f32[1536]{0:T(1024)}) all-reduce(f32[2,384]{1,0:T(2,128)S(1)} %pad_maximum_fusion.1, f32[1536]{0:T(1024)S(1)} %copy-done.23), channel_id=1, replica_groups=mesh['dp'=16,'tensor'=2] {'dp'}, use_global_device_ids=true, to_apply=%region_23.24 | all-reduce | flops 2304 | bytes 18432 | tf_op jit(solution)/shard_map/psum | solution.py:261
  746.2 5.3 convert_element_type.130
  751.6 200.0 %all-reduce.5.cloned.1.call-done = (f32[768,3,384]{2,0,1:T(8,128)}, f32[384,768]{1,0:T(8,128)}, f32[768,1536]{1,0:T(8,128)}, f32[1536,768]{1,0:T(8,128)}) async-done(((f32[768,3,384]{2,0,1:T(8,128)}, f32[384,768]{1,0:T(8,128)}, f32[768,1536]{1,0:T(8,128)}, f32[1536,768]{1,0:T(8,128)}), (f32[768,3,384]{2,0,1:T(8,128)}, f32[384,768]{1,0:T(8,128)}, f32[768,1536]{1,0:T(8,128)}, ...) | async-done | bytes 14155792 | tf_op jit(solution)/shard_map/psum | solution.py:261
  953.2 5.1 copy.111
  959.4 2.4 copy.113
  (214 shorter events, 110.3 us)
Async XLA Ops:
  7.2 201.2 %copy-start = (bf16[768,1536]{1,0:T(8,128)(2,1)S(1)}, bf16[768,1536]{1,0:T(8,128)(2,1)}, u32[]{:S(2)}) copy-start(bf16[768,1536]{1,0:T(8,128)(2,1)} %param.28) | copy-start | bytes 7077892
  7.2 149.8 %reduce-scatter.5.cloned.1.call-start = ((), (), s32[]{:S(2)}) async-start(), calls=%async_computation.4 | async-start | bytes 9437184 | tf_op jit(solution)/shard_map/reduce_scatter | solution.py:180
  10.6 10.6 %copy-start.16 = (s32[2048]{0:T(1024)}, s32[2048]{0:T(1024)S(1)}, u32[]{:S(2)}) copy-start(s32[2048]{0:T(1024)S(1)} %get-tuple-element.152) | copy-start | bytes 24580
  77.1 79.9 %copy-start.24 = (f32[768]{0:T(1024)S(1)}, f32[768]{0:T(1024)}, u32[]{:S(2)}) copy-start(f32[768]{0:T(1024)} %param.25) | copy-start | bytes 9220
  77.1 131.2 %all-gather.6.cloned.1.call-start = ((), (), s32[]{:S(2)}) async-start(), calls=%async_computation.5 | async-start | bytes 4718592 | tf_op jit(solution)/shard_map/all_gather | solution.py:189
  159.8 1.7 copy-start.2
  159.9 1.7 copy-start.15
  159.9 1.6 copy-start.19
  161.5 46.8 %copy-start.29 = (f32[1536]{0:T(1024)S(1)}, f32[1536]{0:T(1024)}, u32[]{:S(2)}) copy-start(f32[1536]{0:T(1024)} %param.29) | copy-start | bytes 18436
  163.2 130.8 %reduce-scatter.7.cloned.1.call-start = ((), (), s32[]{:S(2)}) async-start(), calls=%async_computation.6 | async-start | bytes 4718592 | tf_op jit(solution)/shard_map/reduce_scatter | solution.py:192
  208.3 35.8 %copy-start.28 = (bf16[1536,768]{1,0:T(8,128)(2,1)S(1)}, bf16[1536,768]{1,0:T(8,128)(2,1)}, u32[]{:S(2)}) copy-start(bf16[1536,768]{1,0:T(8,128)(2,1)} %param.30) | copy-start | bytes 7077892
  241.5 2.6 copy-start.30
  250.5 0.7 copy-start.17
  250.5 0.7 copy-start.18
  250.5 43.5 %copy-start.25 = (f32[768]{0:T(1024)S(1)}, f32[768]{0:T(1024)}, u32[]{:S(2)}) copy-start(f32[768]{0:T(1024)} %param.31) | copy-start | bytes 9220
  250.5 100.5 %all-gather.10.cloned.1.call-start = ((), (), s32[]{:S(2)}) async-start(), calls=%async_computation.8 | async-start | bytes 4718592 | tf_op jit(solution)/shard_map/all_gather | solution.py:210
  297.5 1.9 copy-start.7
  297.5 1.9 copy-start.20
  298.0 4.0 copy-start.10
  298.0 4.0 copy-start.26
  306.0 110.4 %reduce-scatter.9.cloned.1.call-start = ((), (), s32[]{:S(2)}) async-start(), calls=%async_computation.9 | async-start | bytes 4718592 | tf_op jit(solution)/shard_map/reduce_scatter | solution.py:216
  363.7 2.7 copy-start.31
  372.8 43.5 %copy-start.3 = (f32[1024,768]{1,0:T(8,128)S(1)}, f32[1024,768]{1,0:T(8,128)}, u32[]{:S(2)}) copy-start(f32[1024,768]{1,0:T(8,128)} %copy-done.2) | copy-start | bytes 9437188
  372.8 96.7 %all-gather.12.cloned.1.call-start = ((), (), s32[]{:S(2)}) async-start(), calls=%async_computation.10 | async-start | bytes 4718592 | tf_op jit(solution)/shard_map/all_gather | solution.py:226
  416.3 3.6 copy-start.6
  416.3 3.8 copy-start.8
  421.5 1.7 copy-start.4
  423.1 46.4 %copy-start.14 = (bf16[384,768]{1,0:T(8,128)(2,1)S(1)}, bf16[384,768]{1,0:T(8,128)(2,1)}, u32[]{:S(2)}) copy-start(bf16[384,768]{1,0:T(8,128)(2,1)} %param.24) | copy-start | bytes 1769476
  424.4 168.5 %reduce-scatter.11.cloned.1.call-start = ((), (), s32[]{:S(2)}) async-start(), calls=%async_computation.11 | async-start | bytes 4718592 | tf_op jit(solution)/shard_map/reduce_scatter | solution.py:240
  534.8 6.8 copy-start.12
  549.5 43.5 %copy-start.5 = (f32[1024,768]{1,0:T(8,128)S(1)}, f32[1024,768]{1,0:T(8,128)}, u32[]{:S(2)}) copy-start(f32[1024,768]{1,0:T(8,128)} %copy-done.4) | copy-start | bytes 9437188
  549.5 90.0 %all-gather.8.cloned.1.call-start = ((), (), s32[]{:S(2)}) async-start(), calls=%async_computation.7 | async-start | bytes 4718592 | tf_op jit(solution)/shard_map/all_gather | solution.py:202
  550.2 196.0 %all-gather.14.cloned.1.call-start = ((), (), s32[]{:S(2)}) async-start(), calls=%async_computation.12 | async-start | bytes 4718592 | tf_op jit(solution)/shard_map/all_gather | solution.py:247
  596.7 10.0 %copy-start.27 = (bf16[2048,768]{1,0:T(8,128)(2,1)S(1)}, bf16[2048,768]{1,0:T(8,128)(2,1)}, u32[]{:S(2)}) copy-start(bf16[2048,768]{1,0:T(8,128)(2,1)} %all-gather.6.cloned.1.call-done) | copy-start | bytes 9437188
  596.7 354.9 %all-reduce.5.cloned.1.call-start = ((), (), s32[]{:S(2)}) async-start(), calls=%async_computation.13 | async-start | bytes 28311552 | tf_op jit(solution)/shard_map/psum | solution.py:261
  596.7 19.7 %slice-start.4 = ((s8[4718592]{0:T(1024)(128)(4,1)}), s8[4194304]{0:T(1024)(128)(4,1)S(1)}, s32[]{:S(2)}) async-start(s8[4718592]{0:T(1024)(128)(4,1)} %bitcast.156), calls=%async_computation.18 | async-start | bytes 8388608
  606.7 9.7 %slice-start.5 = ((s8[4718592]{0:T(1024)(128)(4,1)}), s8[524288]{0:T(1024)(128)(4,1)S(1)}, s32[]{:S(2)}) async-start(s8[4718592]{0:T(1024)(128)(4,1)} %bitcast.156), calls=%async_computation.19 | async-start | bytes 1048576
  606.7 9.7 %copy-start.11 = (bf16[2048,768]{1,0:T(8,128)(2,1)S(1)}, bf16[2048,768]{1,0:T(8,128)(2,1)}, u32[]{:S(2)}) copy-start(bf16[2048,768]{1,0:T(8,128)(2,1)} %param.21) | copy-start | bytes 9437188
  628.2 11.3 %copy-start.21 = (f32[768]{0:T(1024)S(1)}, f32[768]{0:T(1024)}, u32[]{:S(2)}) copy-start(f32[768]{0:T(1024)} %get-tuple-element.144) | copy-start | bytes 9220
  628.2 11.3 %copy-start.22 = (f32[768]{0:T(1024)S(1)}, f32[768]{0:T(1024)}, u32[]{:S(2)}) copy-start(f32[768]{0:T(1024)} %get-tuple-element.149) | copy-start | bytes 9220
  628.2 54.8 %copy-start.23 = (f32[1536]{0:T(1024)S(1)}, f32[1536]{0:T(1024)}, u32[]{:S(2)}) copy-start(f32[1536]{0:T(1024)} %get-tuple-element.221) | copy-start | bytes 18436
  746.2 205.3 %copy-start.9 = (bf16[2048,768]{1,0:T(8,128)(2,1)S(1)}, bf16[2048,768]{1,0:T(8,128)(2,1)}, u32[]{:S(2)}) copy-start(bf16[2048,768]{1,0:T(8,128)(2,1)} %all-gather.8.cloned.1.call-done) | copy-start | bytes 9437188
  951.6 7.8 slice-start.2
  953.2 5.1 copy-start.13
  953.2 6.1 slice-start.3
  958.3 4.2 slice-start
  959.4 3.5 slice-start.1
  959.4 5.7 copy-start.1
Sparse Core Ops, SparseCore 0:
  77.2 79.7 reduce-scatter.4
  163.4 44.9 all-gather.5
  250.6 43.3 reduce-scatter.6
  306.1 44.9 all-gather.9
  372.9 43.3 reduce-scatter.8
  424.6 44.9 all-gather.11
  549.6 43.3 reduce-scatter.10
  594.5 44.9 all-gather.7
  641.6 45.8 all-gather.13
  692.5 259.0 all-reduce.4
where the time goes:
time: 982 us; the launch traced here: 972 us
  waiting for transfers between devices  556 us (57%)
  matrix products  152 us (15%)
  blocking collectives  104 us (11%)
  local copies, waits for them, and re-layouts  85.6 us (9%)
  other arithmetic  57.9 us (6%)
  between operations  15.5 us (2%)
    psum x1, waiting for transfers between devices, body(): lax.psum((qkv_grad, qv_bias_grad, proj_grad, up_grad, up_bias_grad, down_...  200 us
    reduce_scatter x1, waiting for transfers between devices, body(): lax.psum_scatter(jnp.dot(context, proj_weight, preferred_element_type=jnp...  79.8 us
    psum x1, blocking collectives, body(): lax.psum((qkv_grad, qv_bias_grad, proj_grad, up_grad, up_bias_grad, down_...  63.2 us
    all_gather x1, waiting for transfers between devices, body(): lax.all_gather(hidden.astype(jnp.bfloat16), 'tensor', axis=0, tiled=True)  45.1 us
    all_gather x1, waiting for transfers between devices, body(): lax.all_gather(grad_second.astype(jnp.bfloat16), 'tensor', axis=0, tiled=...  45 us
    all_gather x1, waiting for transfers between devices, body(): lax.all_gather(grad_first.astype(jnp.bfloat16), 'tensor', axis=0, tiled=T...  45 us
    reduce_scatter x1, waiting for transfers between devices, body(): lax.psum_scatter(dot_last(grad_pre, up_weight).astype(jnp.bfloat16), 'ten...  43.5 us
    reduce_scatter x1, waiting for transfers between devices, body(): lax.psum_scatter(dot_last(grad_qkv, qkv_flat).astype(jnp.bfloat16), 'tens...  42.7 us
  transfers between devices with their start and end apart: 10, of which 9 were waited for; matrix products, arithmetic and copies ran while one was open for 4% of the time, Pallas kernels for 0%

commit v1 on v0

--- a/solution.py
+++ b/solution.py
@@ -248,15 +248,18 @@
         grad_input_own.astype(jnp.bfloat16), "tensor", axis=0, tiled=True
     ).astype(grad_input_own.dtype)
     norm_sums = lax.psum(
-        (
-            proj_bias_grad,
-            gain_one_grad,
-            shift_one_grad,
-            down_bias_grad,
-            gain_two_grad,
-            shift_two_grad,
+        lax.psum(
+            (
+                proj_bias_grad,
+                gain_one_grad,
+                shift_one_grad,
+                down_bias_grad,
+                gain_two_grad,
+                shift_two_grad,
+            ),
+            "tensor",
         ),
-        ("dp", "tensor"),
+        "dp",
     )
     qkv_grad, qv_bias_grad, proj_grad, up_grad, up_bias_grad, down_grad = lax.psum(
         (qkv_grad, qv_bias_grad, proj_grad, up_grad, up_bias_grad, down_grad), "dp"

time: 982 us -> 981 us (level)
  blocking collectives: 104 us -> 67.1 us
  waiting for transfers between devices: 556 us -> 591 us
    psum x1, waiting for transfers between devices: 200 us -> 235 us  [body(): lax.psum((qkv_grad, qv_bias_grad, proj_grad, up_grad, up_bias_grad, down_...]
    psum x1, blocking collectives: 40.4 us -> 7.1 us  [body(): lax.psum((proj_bias_grad, gain_one_grad, shift_one_grad, down_bias_grad,...]
  transfers between devices with their start and end apart: 10 -> 10, of which waited for: 9 -> 9; matrix products, arithmetic and copies ran while one was open for 4% -> 5% of each run, Pallas kernels for 0% -> 0%
where the time goes in v1:
time: 981 us; the launch traced here: 971 us
  waiting for transfers between devices  591 us (60%)
  matrix products  152 us (15%)
  local copies, waits for them, and re-layouts  85.6 us (9%)
  blocking collectives  67.1 us (7%)
  other arithmetic  58.3 us (6%)
  between operations  15.5 us (2%)
    psum x1, waiting for transfers between devices, body(): lax.psum((qkv_grad, qv_bias_grad, proj_grad, up_grad, up_bias_grad, down_...  235 us
    reduce_scatter x1, waiting for transfers between devices, body(): lax.psum_scatter(jnp.dot(context, proj_weight, preferred_element_type=jnp...  79.8 us
    psum x1, blocking collectives, body(): lax.psum((qkv_grad, qv_bias_grad, proj_grad, up_grad, up_bias_grad, down_...  60 us
    all_gather x1, waiting for transfers between devices, body(): lax.all_gather(hidden.astype(jnp.bfloat16), 'tensor', axis=0, tiled=True)  45.1 us
    all_gather x1, waiting for transfers between devices, body(): lax.all_gather(grad_second.astype(jnp.bfloat16), 'tensor', axis=0, tiled=...  45 us
    all_gather x1, waiting for transfers between devices, body(): lax.all_gather(grad_first.astype(jnp.bfloat16), 'tensor', axis=0, tiled=T...  45 us
    reduce_scatter x1, waiting for transfers between devices, body(): lax.psum_scatter(dot_last(grad_pre, up_weight).astype(jnp.bfloat16), 'ten...  43.5 us
    reduce_scatter x1, waiting for transfers between devices, body(): lax.psum_scatter(dot_last(grad_qkv, qkv_flat).astype(jnp.bfloat16), 'tens...  42.7 us
  transfers between devices with their start and end apart: 10, of which 9 were waited for; matrix products, arithmetic and copies ran while one was open for 5% of the time, Pallas kernels for 0%

profile of v1, /device:TPU:0, one launch (start us, length us, event | category | flops | bytes accessed | tf_op | source)
XLA Modules:
  0.0 970.9 jit_solution(15084983017677057927)
XLA Ops:
  10.6 3.8 copy.62
  14.4 6.7 add_convert_fusion
  21.2 2.3 fusion.69
  23.5 2.7 copy.65
  26.2 2.7 copy.64
  28.8 2.6 copy.63
  33.7 37.3 %while.22 = (s32[]{:T(128)}, bf16[4,512,384]{2,1,0:T(8,128)(2,1)}, f32[4,6,512]{2,1,0:T(8,128)}, bf16[4,512,384]{1,2,0:T(8,128)(2,1)}, pred[4,512,512]{1,2,0:T(8...) while((s32[]{:T(128)}, bf16[4,512,384]{2,1,0:T(8,128)(2,1)}, ...), condition=%wide.region_5.6_spmd, body=%wide.region_2.5_spmd.sunk | while | flops 421721088 | bytes 25792624 | solution.py:178
  71.0 6.0 fusion.72
  77.2 79.8 %reduce-scatter.5.cloned.1.call-done = f32[1024,768]{1,0:T(8,128)} async-done(((f32[2048,768]{1,0:T(8,128)}), f32[1024,768]{1,0:T(8,128)}) %reduce-scatter.5.cloned.1.call-update) | async-done | bytes 3145744 | tf_op jit(solution)/shard_map/reduce_scatter | solution.py:180
  157.0 2.8 fusion.67
  163.3 45.1 %all-gather.6.cloned.1.call-done = bf16[2048,768]{1,0:T(8,128)(2,1)} async-done(((bf16[1024,768]{1,0:T(8,128)(2,1)}), bf16[2048,768]{1,0:T(8,128)(2,1)}) %all-gather.6.cloned.1.call-update) | async-done | bytes 3145744 | tf_op jit(solution)/shard_map/all_gather | solution.py:189
  208.3 33.2 %fusion.20 = (bf16[2048,1536]{1,0:T(8,128)(2,1)S(1)}, f32[2048,1536]{1,0:T(8,128)}) fusion(f32[1536]{0:T(1024)S(1)} %copy-done.29, bf16[2048,768]{1,0:T(8,128)(2,1)} %all-gather.6.cloned.1.call-done, bf16[768,1536]{1,0:T(8,128)(2,1)S(1)} %copy-done), kind=kOutput, calls=%fused_computation.40 | convolution fusion | flops 5039456256 | bytes 24385536 | tf_op jit(solution)/shard_map/dot_general | solution.py:190
  241.5 2.6 copy-done.30
  244.1 6.3 convolution_convert_fusion.2
  251.3 42.7 %reduce-scatter.7.cloned.1.call-done = bf16[1024,768]{1,0:T(8,128)(2,1)} async-done(((bf16[2048,768]{1,0:T(8,128)(2,1)}), bf16[1024,768]{1,0:T(8,128)(2,1)}) %reduce-scatter.7.cloned.1.call-update) | async-done | bytes 1572880 | tf_op jit(solution)/shard_map/reduce_scatter | solution.py:192
  294.0 3.5 fusion.66
  299.4 2.6 fusion.45
  302.0 3.9 fusion.64
  306.0 45.0 %all-gather.10.cloned.1.call-done = bf16[2048,768]{1,0:T(8,128)(2,1)} async-done(((bf16[1024,768]{1,0:T(8,128)(2,1)}), bf16[2048,768]{1,0:T(8,128)(2,1)}) %all-gather.10.cloned.1.call-update) | async-done | bytes 3145744 | tf_op jit(solution)/shard_map/all_gather | solution.py:210
  351.0 12.6 %convert_reduce_fusion = (f32[1536]{0:T(1024)}, bf16[2048,1536]{1,0:T(8,128)(2,1)S(1)}) fusion(f32[2048,1536]{1,0:T(8,128)} %get-tuple-element.226, f32[1536]{0:T(1024)S(1)} %copy-done.29, bf16[2048,768]{1,0:T(8,128)(2,1)} %all-gather.10.cloned.1.call-done, bf16[1536,768]{1,0:T(8,128)(2,1)} %param.30), kind=kOutput, calls=%fused_computation.47 | convolution fusion | flops 4872731136 | bytes 24391680 | tf_op jit(solution)/shard_map/dot_general | solution.py:13
  363.7 2.7 copy-done.31
  366.4 6.4 convolution_convert_fusion.1
  372.9 43.5 %reduce-scatter.9.cloned.1.call-done = bf16[1024,768]{1,0:T(8,128)(2,1)} async-done(((bf16[2048,768]{1,0:T(8,128)(2,1)}), bf16[1024,768]{1,0:T(8,128)(2,1)}) %reduce-scatter.9.cloned.1.call-update) | async-done | bytes 1572880 | tf_op jit(solution)/shard_map/reduce_scatter | solution.py:216
  416.3 3.6 multiply_reduce_fusion.1
  424.5 45.0 %all-gather.12.cloned.1.call-done = bf16[2048,768]{1,0:T(8,128)(2,1)} async-done(((bf16[1024,768]{1,0:T(8,128)(2,1)}), bf16[2048,768]{1,0:T(8,128)(2,1)}) %all-gather.12.cloned.1.call-update) | async-done | bytes 3145744 | tf_op jit(solution)/shard_map/all_gather | solution.py:226
  469.5 4.9 convolution_convert_fusion.3
  474.4 60.4 %while.23 = (s32[]{:T(128)}, bf16[4,512,1152]{1,2,0:T(8,128)(2,1)}, bf16[4,512,384]{1,2,0:T(8,128)(2,1)}, pred[4,512,512]{1,2,0:T(8,128)(4,1)}, bf16[4,512,384]{...) while((s32[]{:T(128)}, bf16[4,512,1152]{1,2,0:T(8,128)(2,1)}, ...), condition=%wide.region_19.20_spmd, body=%wide.region_17.19_spmd.sunk | while | flops 1034744832 | bytes 58806396 | solution.py:229
  482.7 2.3 multiply_reduce_fusion.7
  497.7 2.3 multiply_reduce_fusion.7
  512.7 2.3 multiply_reduce_fusion.7
  527.7 2.3 multiply_reduce_fusion.7
  534.8 6.7 copy.71
  541.5 7.9 convolution_convert_fusion
  550.3 42.7 %reduce-scatter.11.cloned.1.call-done = bf16[1024,768]{1,0:T(8,128)(2,1)} async-done(((bf16[2048,768]{1,0:T(8,128)(2,1)}), bf16[1024,768]{1,0:T(8,128)(2,1)}) %reduce-scatter.11.cloned.1.call-update) | async-done | bytes 1572880 | tf_op jit(solution)/shard_map/reduce_scatter | solution.py:240
  593.0 3.7 fusion.48
  596.8 9.9 %fusion.76 = f32[1536,768]{1,0:T(8,128)} fusion(bf16[2048,1536]{1,0:T(8,128)(2,1)} %copy-done.30, bf16[2048,768]{1,0:T(8,128)(2,1)} %all-gather.10.cloned.1.call-done), kind=kOutput, calls=%fused_computation.151 | convolution fusion | flops 4831838208 | bytes 14155776 | tf_op jit(solution)/shard_map/dot_general | solution.py:19
  606.7 9.7 %fusion.75 = f32[768,1536]{1,0:T(8,128)} fusion(bf16[2048,768]{1,0:T(8,128)(2,1)S(1)} %copy-done.27, bf16[2048,1536]{1,0:T(8,128)(2,1)} %copy-done.31), kind=kOutput, calls=%fused_computation.150 | convolution fusion | flops 4831838208 | bytes 14155776 | tf_op jit(solution)/shard_map/dot_general | solution.py:19
  616.4 4.0 fusion.73
  620.4 2.9 copy.72
  623.4 4.8 fusion.74
  628.2 11.3 %all-gather.8.cloned.1.call-done = bf16[2048,768]{1,0:T(8,128)(2,1)} async-done(((bf16[1024,768]{1,0:T(8,128)(2,1)}), bf16[2048,768]{1,0:T(8,128)(2,1)}) %all-gather.8.cloned.1.call-update) | async-done | bytes 3145744 | tf_op jit(solution)/shard_map/all_gather | solution.py:202
  639.5 7.1 all-reduce.2
  646.6 3.6 convert_reduce_fusion.1
  650.2 60.0 %all-reduce = (f32[2,384]{1,0:T(2,128)}, f32[768]{0:T(1024)}, f32[768]{0:T(1024)}, f32[768]{0:T(1024)}, f32[1536]{0:T(1024)}, /*index=5*/f32[768]{0:T(1024)}, f32[768]{0:T(1024)}, f32[768]{0:T(1024)}) all-reduce(f32[2,384]{1,0:T(2,128)S(1)} %pad_maximum_fusion.1, ...), channel_id=1, replica_groups=mesh['dp'=16,'tensor'=2] {'dp'}, use_global_device_ids=true, to_apply=%region_23.24 | all-reduce | flops 6912 | bytes 55296 | tf_op jit(solution)/shard_map/psum | solution.py:264
  710.2 5.3 convert_element_type.130
  715.5 234.9 %all-reduce.5.cloned.1.call-done = (f32[768,3,384]{2,0,1:T(8,128)}, f32[384,768]{1,0:T(8,128)}, f32[768,1536]{1,0:T(8,128)}, f32[1536,768]{1,0:T(8,128)}) async-done(((f32[768,3,384]{2,0,1:T(8,128)}, f32[384,768]{1,0:T(8,128)}, f32[768,1536]{1,0:T(8,128)}, f32[1536,768]{1,0:T(8,128)}), (f32[768,3,384]{2,0,1:T(8,128)}, f32[384,768]{1,0:T(8,128)}, f32[768,1536]{1,0:T(8,128)}, ...) | async-done | bytes 14155792 | tf_op jit(solution)/shard_map/psum | solution.py:264
  952.0 5.1 copy.111
  958.2 2.4 copy.113
  (214 shorter events, 110.3 us)
Async XLA Ops:
  7.2 201.2 %copy-start = (bf16[768,1536]{1,0:T(8,128)(2,1)S(1)}, bf16[768,1536]{1,0:T(8,128)(2,1)}, u32[]{:S(2)}) copy-start(bf16[768,1536]{1,0:T(8,128)(2,1)} %param.28) | copy-start | bytes 7077892
  7.2 149.8 %reduce-scatter.5.cloned.1.call-start = ((), (), s32[]{:S(2)}) async-start(), calls=%async_computation.4 | async-start | bytes 9437184 | tf_op jit(solution)/shard_map/reduce_scatter | solution.py:180
  10.6 10.6 %copy-start.16 = (s32[2048]{0:T(1024)}, s32[2048]{0:T(1024)S(1)}, u32[]{:S(2)}) copy-start(s32[2048]{0:T(1024)S(1)} %get-tuple-element.152) | copy-start | bytes 24580
  77.1 79.9 %copy-start.24 = (f32[768]{0:T(1024)S(1)}, f32[768]{0:T(1024)}, u32[]{:S(2)}) copy-start(f32[768]{0:T(1024)} %param.25) | copy-start | bytes 9220
  77.1 131.2 %all-gather.6.cloned.1.call-start = ((), (), s32[]{:S(2)}) async-start(), calls=%async_computation.5 | async-start | bytes 4718592 | tf_op jit(solution)/shard_map/all_gather | solution.py:189
  159.8 1.7 copy-start.2
  159.9 1.7 copy-start.15
  159.9 1.6 copy-start.19
  161.5 46.8 %copy-start.29 = (f32[1536]{0:T(1024)S(1)}, f32[1536]{0:T(1024)}, u32[]{:S(2)}) copy-start(f32[1536]{0:T(1024)} %param.29) | copy-start | bytes 18436
  163.2 130.8 %reduce-scatter.7.cloned.1.call-start = ((), (), s32[]{:S(2)}) async-start(), calls=%async_computation.6 | async-start | bytes 4718592 | tf_op jit(solution)/shard_map/reduce_scatter | solution.py:192
  208.3 35.8 %copy-start.28 = (bf16[1536,768]{1,0:T(8,128)(2,1)S(1)}, bf16[1536,768]{1,0:T(8,128)(2,1)}, u32[]{:S(2)}) copy-start(bf16[1536,768]{1,0:T(8,128)(2,1)} %param.30) | copy-start | bytes 7077892
  241.5 2.6 copy-start.30
  250.5 0.7 copy-start.17
  250.5 0.7 copy-start.18
  250.5 43.5 %copy-start.25 = (f32[768]{0:T(1024)S(1)}, f32[768]{0:T(1024)}, u32[]{:S(2)}) copy-start(f32[768]{0:T(1024)} %param.31) | copy-start | bytes 9220
  250.5 100.5 %all-gather.10.cloned.1.call-start = ((), (), s32[]{:S(2)}) async-start(), calls=%async_computation.8 | async-start | bytes 4718592 | tf_op jit(solution)/shard_map/all_gather | solution.py:210
  297.5 1.9 copy-start.7
  297.5 1.9 copy-start.20
  298.0 4.0 copy-start.10
  298.0 4.0 copy-start.26
  306.0 110.4 %reduce-scatter.9.cloned.1.call-start = ((), (), s32[]{:S(2)}) async-start(), calls=%async_computation.9 | async-start | bytes 4718592 | tf_op jit(solution)/shard_map/reduce_scatter | solution.py:216
  363.7 2.7 copy-start.31
  372.8 43.5 %copy-start.3 = (f32[1024,768]{1,0:T(8,128)S(1)}, f32[1024,768]{1,0:T(8,128)}, u32[]{:S(2)}) copy-start(f32[1024,768]{1,0:T(8,128)} %copy-done.2) | copy-start | bytes 9437188
  372.8 96.7 %all-gather.12.cloned.1.call-start = ((), (), s32[]{:S(2)}) async-start(), calls=%async_computation.10 | async-start | bytes 4718592 | tf_op jit(solution)/shard_map/all_gather | solution.py:226
  416.3 3.6 copy-start.6
  416.3 3.8 copy-start.8
  421.5 1.7 copy-start.4
  423.1 46.4 %copy-start.14 = (bf16[384,768]{1,0:T(8,128)(2,1)S(1)}, bf16[384,768]{1,0:T(8,128)(2,1)}, u32[]{:S(2)}) copy-start(bf16[384,768]{1,0:T(8,128)(2,1)} %param.24) | copy-start | bytes 1769476
  424.4 168.5 %reduce-scatter.11.cloned.1.call-start = ((), (), s32[]{:S(2)}) async-start(), calls=%async_computation.11 | async-start | bytes 4718592 | tf_op jit(solution)/shard_map/reduce_scatter | solution.py:240
  534.8 6.8 copy-start.12
  549.5 43.5 %copy-start.5 = (f32[1024,768]{1,0:T(8,128)S(1)}, f32[1024,768]{1,0:T(8,128)}, u32[]{:S(2)}) copy-start(f32[1024,768]{1,0:T(8,128)} %copy-done.4) | copy-start | bytes 9437188
  549.5 90.0 %all-gather.8.cloned.1.call-start = ((), (), s32[]{:S(2)}) async-start(), calls=%async_computation.7 | async-start | bytes 4718592 | tf_op jit(solution)/shard_map/all_gather | solution.py:202
  550.2 160.0 %all-gather.14.cloned.1.call-start = ((), (), s32[]{:S(2)}) async-start(), calls=%async_computation.12 | async-start | bytes 4718592 | tf_op jit(solution)/shard_map/all_gather | solution.py:247
  596.7 10.0 %copy-start.27 = (bf16[2048,768]{1,0:T(8,128)(2,1)S(1)}, bf16[2048,768]{1,0:T(8,128)(2,1)}, u32[]{:S(2)}) copy-start(bf16[2048,768]{1,0:T(8,128)(2,1)} %all-gather.6.cloned.1.call-done) | copy-start | bytes 9437188
  596.7 353.7 %all-reduce.5.cloned.1.call-start = ((), (), s32[]{:S(2)}) async-start(), calls=%async_computation.13 | async-start | bytes 28311552 | tf_op jit(solution)/shard_map/psum | solution.py:264
  596.7 19.7 %slice-start.4 = ((s8[4718592]{0:T(1024)(128)(4,1)}), s8[4194304]{0:T(1024)(128)(4,1)S(1)}, s32[]{:S(2)}) async-start(s8[4718592]{0:T(1024)(128)(4,1)} %bitcast.156), calls=%async_computation.18 | async-start | bytes 8388608
  606.7 9.7 %slice-start.5 = ((s8[4718592]{0:T(1024)(128)(4,1)}), s8[524288]{0:T(1024)(128)(4,1)S(1)}, s32[]{:S(2)}) async-start(s8[4718592]{0:T(1024)(128)(4,1)} %bitcast.156), calls=%async_computation.19 | async-start | bytes 1048576
  606.7 9.7 %copy-start.11 = (bf16[2048,768]{1,0:T(8,128)(2,1)S(1)}, bf16[2048,768]{1,0:T(8,128)(2,1)}, u32[]{:S(2)}) copy-start(bf16[2048,768]{1,0:T(8,128)(2,1)} %param.21) | copy-start | bytes 9437188
  628.2 11.3 %copy-start.21 = (f32[768]{0:T(1024)S(1)}, f32[768]{0:T(1024)}, u32[]{:S(2)}) copy-start(f32[768]{0:T(1024)} %get-tuple-element.144) | copy-start | bytes 9220
  628.2 11.3 %copy-start.22 = (f32[768]{0:T(1024)S(1)}, f32[768]{0:T(1024)}, u32[]{:S(2)}) copy-start(f32[768]{0:T(1024)} %get-tuple-element.149) | copy-start | bytes 9220
  628.2 22.0 %copy-start.23 = (f32[1536]{0:T(1024)S(1)}, f32[1536]{0:T(1024)}, u32[]{:S(2)}) copy-start(f32[1536]{0:T(1024)} %get-tuple-element.227) | copy-start | bytes 18436
  710.2 240.2 %copy-start.9 = (bf16[2048,768]{1,0:T(8,128)(2,1)S(1)}, bf16[2048,768]{1,0:T(8,128)(2,1)}, u32[]{:S(2)}) copy-start(bf16[2048,768]{1,0:T(8,128)(2,1)} %all-gather.8.cloned.1.call-done) | copy-start | bytes 9437188
  950.4 7.8 slice-start.2
  952.0 5.1 copy-start.13
  952.0 6.1 slice-start.3
  957.2 4.2 slice-start
  958.2 3.5 slice-start.1
  958.2 5.7 copy-start.1
Sparse Core Ops, SparseCore 0:
  77.2 79.7 reduce-scatter.4
  163.4 44.9 all-gather.5
  250.6 43.3 reduce-scatter.6
  306.1 44.9 all-gather.9
  372.9 43.3 reduce-scatter.8
  424.6 44.9 all-gather.11
  549.6 43.3 reduce-scatter.10
  594.5 44.9 all-gather.7
  641.6 44.9 all-gather.13
  691.6 258.7 all-reduce.4
